TPU v7x, 256 devices: a whole 4x4x8 slice. The times are simulated.
256 devices in a mesh: chan: 32 (over y_lo, z, core), tm: 8 (over y_hi, x).
Axes of the slice: x: 4, y: 4 (y_hi: 2, y_lo: 2; y = y_hi * 2 + y_lo), z: 8, core: 2. Of those that a mesh axis runs over, the one named last changes fastest.
Arguments:
- traces: bfloat16 [256, 6144], P('chan', 'tm'), may hold values from -6 to 6
- validity: int32 [256], P('chan'), may hold values 0 or 1
- owners: int32 [8], replicated, may hold values from 0 to 31
Outputs:
- correlations: float32 [8, 256, 8, 2048], P(None, 'chan', None, 'tm')
All inputs are finite; a program needn't handle non-finite values. No bound on the sum of `validity` on one device may be relied on, other than what follows from the above.
Results may differ from a plain program's by a relative error of at most 0.0003.
Values may be sent and summed in bfloat16 or wider, within the bound.
No kernel may reach another device: no remote copies, remote signals or barrier semaphores. Data moves between devices by JAX's collectives and lax.ppermute only.
A program may use at most 64 MiB of HBM per device.

v0:
```python
import math
import jax
import jax.numpy as jnp
from jax import lax
from jax.sharding import PartitionSpec as P

LAG = 1024


def broadcast(block, axis, holder):
    block = jnp.where(lax.axis_index(axis) == holder, block, jnp.zeros_like(block))
    return lax.psum(block, axis)


def toeplitz(segment, lag_rows, time_cols):
    seg_width = segment.shape[1]
    repeated = jnp.tile(segment, (1, lag_rows + 1))[:, : lag_rows * (seg_width + 1)]
    return repeated.reshape(segment.shape[0], lag_rows, seg_width + 1)[:, :, :time_cols]


def on_device(traces, validity, owners):
    channels_here = traces.shape[0]
    step_count = owners.shape[0]
    receiver = lax.all_gather(traces, "tm", axis=1, tiled=True)
    time_len = receiver.shape[1]
    lag_dev = 2 * LAG // lax.axis_size("tm")
    valid_flags = validity.astype(jnp.bfloat16)

    def fetch_piece(step_number, buffers):
        source_pieces, source_flags = buffers
        fetched, fetched_flags = (
            broadcast(traces, "chan", owners[step_number]),
            broadcast(valid_flags, "chan", owners[step_number]),
        )
        return (
            source_pieces.at[step_number].set(fetched),
            source_flags.at[step_number].set(fetched_flags),
        )

    initial = (
        jnp.zeros((step_count,) + traces.shape, jnp.bfloat16),
        jnp.zeros((step_count, channels_here), jnp.bfloat16),
    )
    source_pieces, source_flags = lax.fori_loop(0, step_count, fetch_piece, initial)
    sources = lax.all_gather(source_pieces, "tm", axis=2, tiled=True)
    padded = jnp.pad(receiver, ((0, 0), (LAG, LAG)))
    offset = lax.axis_index("tm") * lag_dev
    block_len = 512

    def accumulate(block_number, summed):
        begin_at = block_number * block_len
        segment = lax.dynamic_slice_in_dim(padded, begin_at + offset, block_len + lag_dev, 1)
        shifted = toeplitz(segment, lag_dev, block_len)
        source_block = lax.dynamic_slice_in_dim(sources, begin_at, block_len, 2)
        return summed + jnp.einsum(
            "rku,scu->srck", shifted, source_block, preferred_element_type=jnp.float32
        )

    zeros_acc = jnp.zeros((step_count, channels_here, channels_here, lag_dev), jnp.float32)
    summed = lax.fori_loop(0, time_len // block_len, accumulate, zeros_acc)
    pair_weight = (
        validity.astype(jnp.float32)[None, :, None, None]
        * source_flags.astype(jnp.float32)[:, None, :, None]
    )
    return summed * (1.0 / math.sqrt(time_len)) * pair_weight


def solution(mesh):
    placed = (P("chan", "tm"), P("chan"), P())
    return jax.shard_map(
        on_device,
        mesh=mesh,
        in_specs=placed,
        out_specs=P(None, "chan", None, "tm"),
        check_vma=False,
    )
```

profile of v0, /device:TPU:6, one launch (start us, length us, event | category | flops | bytes accessed | tf_op | source)
XLA Modules:
  0.0 1211.4 jit_solution(13575276252941144519)
XLA Ops:
  0.8 891.6 %while.31 = (s32[]{:T(128)}, bf16[8,8,768]{2,1,0:T(8,128)(2,1)S(1)}, bf16[8,8]{1,0:T(8,128)(2,1)S(1)}, s32[8]{0:T(128)}, bf16[8,768]{1,0:T(8,128)(2,1)}, /*index...) while((s32[]{:T(128)}, ...), condition=%wide.region_5.6_spmd, body=%wide.region_0.5_spmd.sunk | while | flops 18488 | bytes 86400 | solution.py:44
  2.7 110.7 %all-reduce.3 = (bf16[1,8,768]{2,1,0:T(8,128)(2,1)S(1)}, bf16[1,8]{1,0:T(2,128)(2,1)S(1)}) all-reduce(bf16[1,8,768]{2,1,0:T(8,128)(2,1)S(1)} %select_bitcast_fusion.2, bf16[1,8]{1,0:T(2,128)(2,1)S(1)} %fusion.11), channel_id=1, replica_groups=mesh['chan'=32,'tm'=8] {'chan'}, use_global_device_ids=true, to_apply=%region_2.2 | all-reduce | flops 6152 | bytes 24608 | tf_op jit(solution)/shard_map/while/body/eval_jaxpr/psum | solution.py:12
  119.6 104.5 %all-reduce.3 = (bf16[1,8,768]{2,1,0:T(8,128)(2,1)S(1)}, bf16[1,8]{1,0:T(2,128)(2,1)S(1)}) all-reduce(bf16[1,8,768]{2,1,0:T(8,128)(2,1)S(1)} %select_bitcast_fusion.2, bf16[1,8]{1,0:T(2,128)(2,1)S(1)} %fusion.11), channel_id=1, replica_groups=mesh['chan'=32,'tm'=8] {'chan'}, use_global_device_ids=true, to_apply=%region_2.2 | all-reduce | flops 6152 | bytes 24608 | tf_op jit(solution)/shard_map/while/body/eval_jaxpr/psum | solution.py:12
  230.8 104.5 %all-reduce.3 = (bf16[1,8,768]{2,1,0:T(8,128)(2,1)S(1)}, bf16[1,8]{1,0:T(2,128)(2,1)S(1)}) all-reduce(bf16[1,8,768]{2,1,0:T(8,128)(2,1)S(1)} %select_bitcast_fusion.2, bf16[1,8]{1,0:T(2,128)(2,1)S(1)} %fusion.11), channel_id=1, replica_groups=mesh['chan'=32,'tm'=8] {'chan'}, use_global_device_ids=true, to_apply=%region_2.2 | all-reduce | flops 6152 | bytes 24608 | tf_op jit(solution)/shard_map/while/body/eval_jaxpr/psum | solution.py:12
  341.4 104.6 %all-reduce.3 = (bf16[1,8,768]{2,1,0:T(8,128)(2,1)S(1)}, bf16[1,8]{1,0:T(2,128)(2,1)S(1)}) all-reduce(bf16[1,8,768]{2,1,0:T(8,128)(2,1)S(1)} %select_bitcast_fusion.2, bf16[1,8]{1,0:T(2,128)(2,1)S(1)} %fusion.11), channel_id=1, replica_groups=mesh['chan'=32,'tm'=8] {'chan'}, use_global_device_ids=true, to_apply=%region_2.2 | all-reduce | flops 6152 | bytes 24608 | tf_op jit(solution)/shard_map/while/body/eval_jaxpr/psum | solution.py:12
  452.0 104.5 %all-reduce.3 = (bf16[1,8,768]{2,1,0:T(8,128)(2,1)S(1)}, bf16[1,8]{1,0:T(2,128)(2,1)S(1)}) all-reduce(bf16[1,8,768]{2,1,0:T(8,128)(2,1)S(1)} %select_bitcast_fusion.2, bf16[1,8]{1,0:T(2,128)(2,1)S(1)} %fusion.11), channel_id=1, replica_groups=mesh['chan'=32,'tm'=8] {'chan'}, use_global_device_ids=true, to_apply=%region_2.2 | all-reduce | flops 6152 | bytes 24608 | tf_op jit(solution)/shard_map/while/body/eval_jaxpr/psum | solution.py:12
  562.6 104.5 %all-reduce.3 = (bf16[1,8,768]{2,1,0:T(8,128)(2,1)S(1)}, bf16[1,8]{1,0:T(2,128)(2,1)S(1)}) all-reduce(bf16[1,8,768]{2,1,0:T(8,128)(2,1)S(1)} %select_bitcast_fusion.2, bf16[1,8]{1,0:T(2,128)(2,1)S(1)} %fusion.11), channel_id=1, replica_groups=mesh['chan'=32,'tm'=8] {'chan'}, use_global_device_ids=true, to_apply=%region_2.2 | all-reduce | flops 6152 | bytes 24608 | tf_op jit(solution)/shard_map/while/body/eval_jaxpr/psum | solution.py:12
  673.2 104.5 %all-reduce.3 = (bf16[1,8,768]{2,1,0:T(8,128)(2,1)S(1)}, bf16[1,8]{1,0:T(2,128)(2,1)S(1)}) all-reduce(bf16[1,8,768]{2,1,0:T(8,128)(2,1)S(1)} %select_bitcast_fusion.2, bf16[1,8]{1,0:T(2,128)(2,1)S(1)} %fusion.11), channel_id=1, replica_groups=mesh['chan'=32,'tm'=8] {'chan'}, use_global_device_ids=true, to_apply=%region_2.2 | all-reduce | flops 6152 | bytes 24608 | tf_op jit(solution)/shard_map/while/body/eval_jaxpr/psum | solution.py:12
  783.7 104.5 %all-reduce.3 = (bf16[1,8,768]{2,1,0:T(8,128)(2,1)S(1)}, bf16[1,8]{1,0:T(2,128)(2,1)S(1)}) all-reduce(bf16[1,8,768]{2,1,0:T(8,128)(2,1)S(1)} %select_bitcast_fusion.2, bf16[1,8]{1,0:T(2,128)(2,1)S(1)} %fusion.11), channel_id=1, replica_groups=mesh['chan'=32,'tm'=8] {'chan'}, use_global_device_ids=true, to_apply=%region_2.2 | all-reduce | flops 6152 | bytes 24608 | tf_op jit(solution)/shard_map/while/body/eval_jaxpr/psum | solution.py:12
  892.3 37.7 %all_gather.6 = bf16[8,8,6144]{2,1,0:T(8,128)(2,1)} all-gather(bf16[8,8,768]{2,1,0:T(8,128)(2,1)S(1)} %get-tuple-element.253), channel_id=1, replica_groups=mesh['chan'=32,'tm'=8] {'tm'}, dimensions={2}, use_global_device_ids=true | all-gather | bytes 884736 | tf_op jit(solution)/shard_map/all_gather | solution.py:45
  930.1 34.4 %all_gather.7 = bf16[8,6144]{1,0:T(8,128)(2,1)S(1)} all-gather(bf16[8,768]{1,0:T(8,128)(2,1)} %get-tuple-element.441), channel_id=1, replica_groups=mesh['chan'=32,'tm'=8] {'tm'}, dimensions={1}, use_global_device_ids=true | all-gather | bytes 110592 | tf_op jit(solution)/shard_map/all_gather | solution.py:24
  964.5 244.9 %while.32 = (s32[]{:T(128)}, f32[8,8,8,256]{3,2,1,0:T(8,128)}, bf16[8,8,6144]{2,1,0:T(8,128)(2,1)}, s32[]{:T(128)}, bf16[8,8192]{1,0:T(8,128)(2,1)S(1)}, /*index...) while((s32[]{:T(128)}, f32[8,8,8,256]{3,2,1,0:T(8,128)}, ...), condition=%wide.region_7.8_spmd.clone, body=%wide.region_6.7_spmd.clone.sunk | while | flops 134479888 | bytes 29499664 | solution.py:60
  971.4 10.3 reshape.131
  991.8 10.3 reshape.131
  1012.2 10.3 reshape.131
  1032.6 10.3 reshape.131
  1053.0 10.3 reshape.131
  1073.4 10.3 reshape.131
  1093.8 10.3 reshape.131
  1114.2 10.3 reshape.131
  1134.6 10.3 reshape.131
  1155.0 10.3 reshape.131
  1175.4 10.3 reshape.131
  1195.8 10.3 reshape.131
  (180 shorter events, 167.7 us)
Async XLA Ops:
  971.4 10.3 copy-start
  984.1 0.8 copy-start.1
  991.8 10.3 copy-start
  1004.5 0.8 copy-start.1
  1012.2 10.3 copy-start
  1025.0 0.8 copy-start.1
  1032.6 10.3 copy-start
  1045.4 0.8 copy-start.1
  1053.0 10.3 copy-start
  1065.8 0.8 copy-start.1
  1073.4 10.3 copy-start
  1086.2 0.8 copy-start.1
  1093.8 10.3 copy-start
  1106.6 0.8 copy-start.1
  1114.2 10.3 copy-start
  1127.0 0.8 copy-start.1
  1134.6 10.3 copy-start
  1147.4 0.8 copy-start.1
  1155.0 10.3 copy-start
  1167.8 0.8 copy-start.1
  1175.4 10.3 copy-start
  1188.2 0.8 copy-start.1
  1195.8 10.3 copy-start
  1208.6 0.8 copy-start.1
where the time goes:
time: 1210 us
  blocking collectives  914 us (76%)
  local copies, waits for them, and re-layouts  226 us (19%)
  other arithmetic  36.3 us (3%)
  matrix products  29.5 us (2%)
    psum x8, blocking collectives, broadcast(): return lax.psum(block, axis)  842 us
    reshape x12, local copies, waits for them, and re-layouts, toeplitz(): repeated.reshape(segment.shape[0], lag_rows, seg_width + 1)  123 us
    while x60, local copies, waits for them, and re-layouts  86 us
    all_gather x1, blocking collectives, on_device(): sources = lax.all_gather(source_pieces, 'tm', axis=2, tiled=True)  37.7 us
    all_gather x1, blocking collectives, on_device(): receiver = lax.all_gather(traces, 'tm', axis=1, tiled=True)  34.4 us
    dot_general x12, matrix products, accumulate(): jnp.einsum('rku,scu->srck', shifted, source_block, preferred_element_type...  29.5 us
    another operation x40, other arithmetic  28.3 us

commit v1 on v0

--- a/solution.py
+++ b/solution.py
@@ -7,9 +7,13 @@
 LAG = 1024
 
 
+def stops_all_switch(mat, link_axis):
+    return jnp.sum(jax.lax.all_gather(mat, link_axis), 0)
+
+
 def broadcast(block, axis, holder):
     block = jnp.where(lax.axis_index(axis) == holder, block, jnp.zeros_like(block))
-    return lax.psum(block, axis)
+    return stops_all_switch(block, axis)
 
 
 def toeplitz(segment, lag_rows, time_cols):

time: 1210 us -> 1080 us (0.89)
  blocking collectives: 914 us -> 769 us
  local copies, waits for them, and re-layouts: 226 us -> 239 us
    psum x8 -> x0, blocking collectives: 842 us -> none  [broadcast(): return lax.psum(block, axis)]
    while x0 -> x8, blocking collectives: none -> 438 us
    all_gather x0 -> x8, blocking collectives: none -> 258 us  [stops_all_switch(): return jnp.sum(jax.lax.all_gather(mat, link_axis), 0)]
    while x60 -> x84, local copies, waits for them, and re-layouts: 86 us -> 98.5 us
    another operation x40 -> x24, other arithmetic: 28.3 us -> 26.4 us
where the time goes in v1:
time: 1080 us
  blocking collectives  769 us (71%)
  local copies, waits for them, and re-layouts  239 us (22%)
  other arithmetic  35.4 us (3%)
  matrix products  29.5 us (3%)
    while x8, blocking collectives  438 us
    all_gather x8, blocking collectives, stops_all_switch(): return jnp.sum(jax.lax.all_gather(mat, link_axis), 0)  258 us
    reshape x12, local copies, waits for them, and re-layouts, toeplitz(): repeated.reshape(segment.shape[0], lag_rows, seg_width + 1)  123 us
    while x84, local copies, waits for them, and re-layouts  98.5 us
    all_gather x1, blocking collectives, on_device(): sources = lax.all_gather(source_pieces, 'tm', axis=2, tiled=True)  37.8 us
    all_gather x1, blocking collectives, on_device(): receiver = lax.all_gather(traces, 'tm', axis=1, tiled=True)  34.4 us
    dot_general x12, matrix products, accumulate(): jnp.einsum('rku,scu->srck', shifted, source_block, preferred_element_type...  29.5 us
    another operation x24, other arithmetic  26.4 us

profile of v1, /device:TPU:6, one launch (start us, length us, event | category | flops | bytes accessed | tf_op | source)
XLA Modules:
  0.0 1082.6 jit_solution(10219744990861748185)
XLA Ops:
  0.8 762.7 %while.34 = (s32[]{:T(128)}, bf16[8,8,768]{2,1,0:T(8,128)(2,1)S(1)}, bf16[8,8]{1,0:T(8,128)(2,1)S(1)}, s32[8]{0:T(128)}, bf16[8,768]{1,0:T(8,128)(2,1)}, /*index...) while((s32[]{:T(128)}, ...), condition=%wide.region_5.6_spmd, body=%wide.region_0.5_spmd.sunk | while | flops 203307 | bytes 876008 | solution.py:48
  2.6 38.3 %all-gather.3 = bf16[256,768]{1,0:T(8,128)(2,1)S(1)} all-gather(bf16[8,768]{1,0:T(8,128)(2,1)S(1)} %broadcast_select_fusion.6), channel_id=2, replica_groups=mesh['chan'=32,'tm'=8] {'chan'}, dimensions={0}, use_global_device_ids=true | all-gather | bytes 405504 | tf_op jit(solution)/shard_map/while/body/eval_jaxpr/all_gather | solution.py:11
  46.5 53.4 %all-reduce.3 = bf16[256]{0:T(256)(128)(2,1)S(1)} all-reduce(bf16[256]{0:T(256)(128)(2,1)S(1)} %dynamic-update-slice.24), channel_id=3, replica_groups=mesh['chan'=32,'tm'=8] {'chan'}, use_global_device_ids=true, to_apply=%add.1 | all-reduce | flops 256 | bytes 1024 | tf_op jit(solution)/shard_map/while
  102.4 31.5 %all-gather.3 = bf16[256,768]{1,0:T(8,128)(2,1)S(1)} all-gather(bf16[8,768]{1,0:T(8,128)(2,1)S(1)} %broadcast_select_fusion.6), channel_id=2, replica_groups=mesh['chan'=32,'tm'=8] {'chan'}, dimensions={0}, use_global_device_ids=true | all-gather | bytes 405504 | tf_op jit(solution)/shard_map/while/body/eval_jaxpr/all_gather | solution.py:11
  139.5 55.0 %all-reduce.3 = bf16[256]{0:T(256)(128)(2,1)S(1)} all-reduce(bf16[256]{0:T(256)(128)(2,1)S(1)} %dynamic-update-slice.24), channel_id=3, replica_groups=mesh['chan'=32,'tm'=8] {'chan'}, use_global_device_ids=true, to_apply=%add.1 | all-reduce | flops 256 | bytes 1024 | tf_op jit(solution)/shard_map/while
  197.7 31.4 %all-gather.3 = bf16[256,768]{1,0:T(8,128)(2,1)S(1)} all-gather(bf16[8,768]{1,0:T(8,128)(2,1)S(1)} %broadcast_select_fusion.6), channel_id=2, replica_groups=mesh['chan'=32,'tm'=8] {'chan'}, dimensions={0}, use_global_device_ids=true | all-gather | bytes 405504 | tf_op jit(solution)/shard_map/while/body/eval_jaxpr/all_gather | solution.py:11
  234.8 55.0 %all-reduce.3 = bf16[256]{0:T(256)(128)(2,1)S(1)} all-reduce(bf16[256]{0:T(256)(128)(2,1)S(1)} %dynamic-update-slice.24), channel_id=3, replica_groups=mesh['chan'=32,'tm'=8] {'chan'}, use_global_device_ids=true, to_apply=%add.1 | all-reduce | flops 256 | bytes 1024 | tf_op jit(solution)/shard_map/while
  292.3 31.5 %all-gather.3 = bf16[256,768]{1,0:T(8,128)(2,1)S(1)} all-gather(bf16[8,768]{1,0:T(8,128)(2,1)S(1)} %broadcast_select_fusion.6), channel_id=2, replica_groups=mesh['chan'=32,'tm'=8] {'chan'}, dimensions={0}, use_global_device_ids=true | all-gather | bytes 405504 | tf_op jit(solution)/shard_map/while/body/eval_jaxpr/all_gather | solution.py:11
  329.3 55.0 %all-reduce.3 = bf16[256]{0:T(256)(128)(2,1)S(1)} all-reduce(bf16[256]{0:T(256)(128)(2,1)S(1)} %dynamic-update-slice.24), channel_id=3, replica_groups=mesh['chan'=32,'tm'=8] {'chan'}, use_global_device_ids=true, to_apply=%add.1 | all-reduce | flops 256 | bytes 1024 | tf_op jit(solution)/shard_map/while
  386.9 31.5 %all-gather.3 = bf16[256,768]{1,0:T(8,128)(2,1)S(1)} all-gather(bf16[8,768]{1,0:T(8,128)(2,1)S(1)} %broadcast_select_fusion.6), channel_id=2, replica_groups=mesh['chan'=32,'tm'=8] {'chan'}, dimensions={0}, use_global_device_ids=true | all-gather | bytes 405504 | tf_op jit(solution)/shard_map/while/body/eval_jaxpr/all_gather | solution.py:11
  423.9 55.0 %all-reduce.3 = bf16[256]{0:T(256)(128)(2,1)S(1)} all-reduce(bf16[256]{0:T(256)(128)(2,1)S(1)} %dynamic-update-slice.24), channel_id=3, replica_groups=mesh['chan'=32,'tm'=8] {'chan'}, use_global_device_ids=true, to_apply=%add.1 | all-reduce | flops 256 | bytes 1024 | tf_op jit(solution)/shard_map/while
  481.5 31.5 %all-gather.3 = bf16[256,768]{1,0:T(8,128)(2,1)S(1)} all-gather(bf16[8,768]{1,0:T(8,128)(2,1)S(1)} %broadcast_select_fusion.6), channel_id=2, replica_groups=mesh['chan'=32,'tm'=8] {'chan'}, dimensions={0}, use_global_device_ids=true | all-gather | bytes 405504 | tf_op jit(solution)/shard_map/while/body/eval_jaxpr/all_gather | solution.py:11
  518.5 55.0 %all-reduce.3 = bf16[256]{0:T(256)(128)(2,1)S(1)} all-reduce(bf16[256]{0:T(256)(128)(2,1)S(1)} %dynamic-update-slice.24), channel_id=3, replica_groups=mesh['chan'=32,'tm'=8] {'chan'}, use_global_device_ids=true, to_apply=%add.1 | all-reduce | flops 256 | bytes 1024 | tf_op jit(solution)/shard_map/while
  576.1 31.5 %all-gather.3 = bf16[256,768]{1,0:T(8,128)(2,1)S(1)} all-gather(bf16[8,768]{1,0:T(8,128)(2,1)S(1)} %broadcast_select_fusion.6), channel_id=2, replica_groups=mesh['chan'=32,'tm'=8] {'chan'}, dimensions={0}, use_global_device_ids=true | all-gather | bytes 405504 | tf_op jit(solution)/shard_map/while/body/eval_jaxpr/all_gather | solution.py:11
  613.1 55.0 %all-reduce.3 = bf16[256]{0:T(256)(128)(2,1)S(1)} all-reduce(bf16[256]{0:T(256)(128)(2,1)S(1)} %dynamic-update-slice.24), channel_id=3, replica_groups=mesh['chan'=32,'tm'=8] {'chan'}, use_global_device_ids=true, to_apply=%add.1 | all-reduce | flops 256 | bytes 1024 | tf_op jit(solution)/shard_map/while
  670.7 31.5 %all-gather.3 = bf16[256,768]{1,0:T(8,128)(2,1)S(1)} all-gather(bf16[8,768]{1,0:T(8,128)(2,1)S(1)} %broadcast_select_fusion.6), channel_id=2, replica_groups=mesh['chan'=32,'tm'=8] {'chan'}, dimensions={0}, use_global_device_ids=true | all-gather | bytes 405504 | tf_op jit(solution)/shard_map/while/body/eval_jaxpr/all_gather | solution.py:11
  707.7 55.0 %all-reduce.3 = bf16[256]{0:T(256)(128)(2,1)S(1)} all-reduce(bf16[256]{0:T(256)(128)(2,1)S(1)} %dynamic-update-slice.24), channel_id=3, replica_groups=mesh['chan'=32,'tm'=8] {'chan'}, use_global_device_ids=true, to_apply=%add.1 | all-reduce | flops 256 | bytes 1024 | tf_op jit(solution)/shard_map/while
  763.4 37.8 %all_gather.34 = bf16[8,8,6144]{2,1,0:T(8,128)(2,1)} all-gather(bf16[8,8,768]{2,1,0:T(8,128)(2,1)S(1)} %get-tuple-element.316), channel_id=1, replica_groups=mesh['chan'=32,'tm'=8] {'tm'}, dimensions={2}, use_global_device_ids=true | all-gather | bytes 884736 | tf_op jit(solution)/shard_map/all_gather | solution.py:49
  801.2 34.4 %all_gather.35 = bf16[8,6144]{1,0:T(8,128)(2,1)S(1)} all-gather(bf16[8,768]{1,0:T(8,128)(2,1)} %get-tuple-element.510), channel_id=1, replica_groups=mesh['chan'=32,'tm'=8] {'tm'}, dimensions={1}, use_global_device_ids=true | all-gather | bytes 110592 | tf_op jit(solution)/shard_map/all_gather | solution.py:28
  835.6 244.9 %while.35 = (s32[]{:T(128)}, f32[8,8,8,256]{3,2,1,0:T(8,128)}, bf16[8,8,6144]{2,1,0:T(8,128)(2,1)}, s32[]{:T(128)}, bf16[8,8192]{1,0:T(8,128)(2,1)S(1)}, /*index...) while((s32[]{:T(128)}, f32[8,8,8,256]{3,2,1,0:T(8,128)}, ...), condition=%wide.region_7.8_spmd.clone, body=%wide.region_6.7_spmd.clone.sunk | while | flops 134479888 | bytes 29499664 | solution.py:64
  924.1 10.3 reshape.184
  964.9 10.3 reshape.184
  1005.8 10.3 reshape.184
  1046.6 10.3 reshape.184
  (236 shorter events, 262.2 us)
Async XLA Ops:
  842.5 10.3 copy-start
  855.3 0.8 copy-start.1
  862.9 10.3 copy-start
  875.7 0.8 copy-start.1
  883.3 10.3 copy-start
  896.1 0.8 copy-start.1
  903.7 10.3 copy-start
  916.5 0.8 copy-start.1
  924.1 10.3 copy-start
  936.9 0.8 copy-start.1
  944.5 10.3 copy-start
  957.3 0.8 copy-start.1
  964.9 10.3 copy-start
  977.7 0.8 copy-start.1
  985.3 10.3 copy-start
  998.1 0.8 copy-start.1
  1005.8 10.3 copy-start
  1018.5 0.8 copy-start.1
  1026.2 10.3 copy-start
  1038.9 0.8 copy-start.1
  1046.6 10.3 copy-start
  1059.3 0.8 copy-start.1
  1067.0 10.3 copy-start
  1079.7 0.8 copy-start.1
